TPU v7x, 32 devices: a whole 2x2x4 slice. The times are simulated.
32 devices in a mesh: groups: 2 (over y), expert: 16 (over z, x, core).
Axes of the slice: x: 2, y: 2, z: 4, core: 2. Of those that a mesh axis runs over, the one named last changes fastest.
Arguments:
- tokens: bfloat16 [4096, 2048], P(('groups', 'expert')), parts along dimension 0, may hold values from -6 to 6
- route_ids: int32 [4096, 8], P(('groups', 'expert')), parts along dimension 0, may hold values from 0 to 15, all different within a row; in each aligned block of 128 rows (0 to 127, 128 to 255, ...) at most 80 rows name the same one
- gates: float32 [4096, 8], P(('groups', 'expert')), parts along dimension 0, may hold values from 0.3 to 1
- w_gate: bfloat16 [16, 2048, 768], P('expert'), may hold values from -0.125 to 0.125
- w_up: bfloat16 [16, 2048, 768], P('expert'), may hold values from -0.125 to 0.125
- w_down: bfloat16 [16, 768, 2048], P('expert'), may hold values from -0.21875 to 0.21875
Outputs:
- combined: bfloat16 [4096, 2048], P(('groups', 'expert')), parts along dimension 0
There are 2 independent parts, one for each index of `groups`. A program takes and returns all parts, laid end to end along the dimension named above; an argument that names none is the same for every part. Nothing has to cross between parts.
Inputs may be any that keep to these rules, and one draw needn't show every extreme that they name: `route_ids`: each row names 8 different experts. In each aligned block of 128 rows (one device's tokens) no expert is named by more than 80 rows, a bound that some block reaches.
All inputs are finite; a program needn't handle non-finite values.
Results may differ from a plain program's by a relative error of at most 0.0058.
Values may be sent and summed in bfloat16 or wider, within the bound.
A program may use at most 128 MiB of HBM per device.

v0:
```python
import jax
import jax.numpy as jnp
from jax import lax
from jax.sharding import PartitionSpec as P


def expert_mlp(block_data, gate_local, up_local, down_local):
    gate_part = jnp.dot(block_data, gate_local, preferred_element_type=jnp.float32)
    up_part = jnp.dot(block_data, up_local, preferred_element_type=jnp.float32)
    hidden = (jax.nn.silu(gate_part) * up_part).astype(jnp.bfloat16)
    return jnp.dot(hidden, down_local, preferred_element_type=jnp.float32)


def dense_on_device(tokens, route_ids, gates, w_gate, w_up, w_down):
    n_peers = lax.axis_size("expert")
    me = lax.axis_index("expert")
    experts = jnp.arange(n_peers, dtype=jnp.int32)
    weight = jnp.sum(
        jnp.where(route_ids[:, None, :] == experts[None, :, None], gates[:, None, :], 0.0), axis=2
    )
    weights = lax.all_gather(weight, "expert", axis=0, tiled=True)
    mine = lax.dynamic_slice_in_dim(weights, me, 1, axis=1)
    everyone = lax.all_gather(tokens, "expert", axis=0, tiled=True)
    part = expert_mlp(everyone, w_gate[0], w_up[0], w_down[0])
    part = part.astype(jnp.bfloat16).astype(jnp.float32) * mine
    return lax.psum_scatter(part.astype(jnp.bfloat16), "expert", scatter_dimension=0, tiled=True)


def routed_on_device(tokens, route_ids, gates, w_gate, w_up, w_down):
    n_peers = lax.axis_size("expert")
    tok_rows, top_k = route_ids.shape
    model_width = tokens.shape[1]
    capacity = 5 * tok_rows * top_k // (4 * n_peers)
    buffer_rows = n_peers * capacity
    assigned = tok_rows * top_k
    chosen = route_ids.reshape(-1)
    onehot = (chosen[:, None] == jnp.arange(n_peers, dtype=jnp.int32)[None, :]).astype(jnp.int32)
    running = jnp.cumsum(onehot, axis=0)
    position = jnp.sum(running * onehot, axis=1) - 1
    slot_of = chosen * capacity + position
    ordinal = jnp.arange(assigned, dtype=jnp.int32)
    anchor = jnp.zeros((buffer_rows,), jnp.int32).at[slot_of].set(ordinal)
    outgoing = tokens[anchor // top_k].reshape(n_peers, capacity, model_width)
    incoming = lax.all_to_all(outgoing, "expert", split_axis=0, concat_axis=0, tiled=True)
    n_src, n_items, _ = incoming.shape
    computed = expert_mlp(
        incoming.reshape(n_src * n_items, model_width), w_gate[0], w_up[0], w_down[0]
    ).astype(jnp.bfloat16)
    computed = computed.reshape(n_src, n_items, model_width)
    returned_rows = lax.all_to_all(computed, "expert", split_axis=0, concat_axis=0, tiled=True)
    returned = returned_rows.reshape(buffer_rows, model_width)[slot_of].astype(jnp.float32)
    combined = jnp.sum(returned.reshape(tok_rows, top_k, model_width) * gates[:, :, None], axis=1)
    return combined.astype(jnp.bfloat16)


def solution(mesh):
    n_peers = mesh.shape["expert"]

    def on_device(tokens, route_ids, gates, w_gate, w_up, w_down):
        dense = n_peers <= 4 * route_ids.shape[1]
        body = dense_on_device if dense else routed_on_device
        return body(tokens, route_ids, gates, w_gate, w_up, w_down)

    in_specs = (
        P(("groups", "expert"), None),
        P(("groups", "expert"), None),
        P(("groups", "expert"), None),
        P("expert", None, None),
        P("expert", None, None),
        P("expert", None, None),
    )
    out_specs = P(("groups", "expert"), None)
    return jax.shard_map(
        on_device, mesh=mesh, in_specs=in_specs, out_specs=out_specs, check_vma=False
    )
```

profile of v0, /device:TPU:0, one launch (start us, length us, event | category | flops | bytes accessed | tf_op | source)
XLA Modules:
  0.0 228.0 jit_solution(3535841203120528709)
XLA Ops:
  6.5 0.0 copy-start
  6.5 0.0 all-gather.2.cloned.1.call-start
  6.5 0.7 all-gather.2.cloned.1.call-update
  7.3 0.0 reduce-scatter.2.cloned.1.call-start
  7.3 0.9 select_reduce_fusion
  8.2 24.1 %all_gather.7 = f32[2048,16]{0,1:T(8,128)S(1)} all-gather(f32[128,16]{0,1:T(8,128)S(1)} %select_reduce_fusion), channel_id=1, replica_groups=mesh['groups'=2,'expert'=16] {'expert'}, dimensions={0}, use_global_device_ids=true | all-gather | bytes 139264 | tf_op jit(solution)/shard_map/all_gather | solution.py:21
  32.3 54.4 %all-gather.2.cloned.1.call-done = bf16[2048,2048]{1,0:T(8,128)(2,1)} async-done(((bf16[128,2048]{1,0:T(8,128)(2,1)}), bf16[2048,2048]{1,0:T(8,128)(2,1)}) %all-gather.2.cloned.1.call-update) | async-done | bytes 8388624 | tf_op jit(solution)/shard_map/all_gather | solution.py:23
  86.7 11.7 %fusion.3 = f32[2048,768]{1,0:T(8,128)} fusion(bf16[2048,2048]{1,0:T(8,128)(2,1)} %all-gather.2.cloned.1.call-done, bf16[1,2048,768]{2,1,0:T(8,128)(2,1)} %param.9), kind=kOutput, calls=%fused_computation.4 | convolution fusion | flops 6442450944 | bytes 17825792 | tf_op jit(solution)/shard_map/dot_general | solution.py:8
  98.4 0.0 copy-done
  98.4 20.6 %multiply_convert_fusion = bf16[2048,2048]{1,0:T(8,128)(2,1)} fusion(f32[2048]{0:T(1024)S(1)} %bitcast.13, f32[2048,768]{1,0:T(8,128)} %fusion.3, bf16[2048,2048]{1,0:T(8,128)(2,1)} %all-gather.2.cloned.1.call-done, bf16[1,768,2048]{2,1,0:T(8,128)(2,1)S(1)} %copy-done, bf16[1,2048,768]{2,1,0:T(8,128)(2,1)} %param.10), kind=kOutput, calls=%fused_computation | convolution fusion | flops 12911116288 | bytes 29368320 | tf_op jit(solution)/shard_map/dot_general | solution.py:11
  119.0 0.0 reduce-scatter.2.cloned.1.call-update
  119.0 102.2 %reduce-scatter.2.cloned.1.call-done = bf16[128,2048]{1,0:T(8,128)(2,1)} async-done(((bf16[2048,2048]{1,0:T(8,128)(2,1)}), bf16[128,2048]{1,0:T(8,128)(2,1)}) %reduce-scatter.2.cloned.1.call-update) | async-done | bytes 524304 | tf_op jit(solution)/shard_map/reduce_scatter | solution.py:26
  (1 shorter events, 0.0 us)
Async XLA Ops:
  6.5 91.9 %copy-start = (bf16[1,768,2048]{2,1,0:T(8,128)(2,1)S(1)}, bf16[1,768,2048]{2,1,0:T(8,128)(2,1)}, u32[]{:S(2)}) copy-start(bf16[1,768,2048]{2,1,0:T(8,128)(2,1)} %param.11) | copy-start | bytes 9437188
  6.5 80.2 %all-gather.2.cloned.1.call-start = ((), (), s32[]{:S(2)}) async-start(), calls=%async_computation.1 | async-start | bytes 8912896 | tf_op jit(solution)/shard_map/all_gather | solution.py:23
  7.3 213.9 %reduce-scatter.2.cloned.1.call-start = ((), (), s32[]{:S(2)}) async-start(), calls=%async_computation.2 | async-start | bytes 8912896 | tf_op jit(solution)/shard_map/reduce_scatter | solution.py:26
Sparse Core Ops, SparseCore 0:
  9.5 77.1 all-gather.1
  119.1 102.0 reduce-scatter.1
where the time goes:
time: 228 us
  waiting for transfers between devices  157 us (69%)
  matrix products  32.3 us (14%)
  blocking collectives  24.1 us (11%)
  between operations  13.4 us (6%)
    reduce_scatter x1, waiting for transfers between devices, dense_on_device(): lax.psum_scatter(part.astype(jnp.bfloat16), 'expert', scatter_dimension=0...  102 us
    all_gather x1, waiting for transfers between devices, dense_on_device(): everyone = lax.all_gather(tokens, 'expert', axis=0, tiled=True)  54.4 us
    all_gather x1, blocking collectives, dense_on_device(): weights = lax.all_gather(weight, 'expert', axis=0, tiled=True)  24.1 us
    dot_general x1, matrix products, expert_mlp(): return jnp.dot(hidden, down_local, preferred_element_type=jnp.float32)  20.6 us
    dot_general x1, matrix products, expert_mlp(): jnp.dot(block_data, gate_local, preferred_element_type=jnp.float32)  11.7 us
  transfers between devices with their start and end apart: 2, of which 2 were waited for; matrix products, arithmetic and copies ran while one was open for 0% of the time, Pallas kernels for 0%

commit v1 on v0

--- a/solution.py
+++ b/solution.py
@@ -2,6 +2,7 @@
 import jax.numpy as jnp
 from jax import lax
 from jax.sharding import PartitionSpec as P
+from jax.lax import axis_index, axis_size, ppermute
 
 
 def expert_mlp(block_data, gate_local, up_local, down_local):
@@ -20,7 +21,17 @@
     )
     weights = lax.all_gather(weight, "expert", axis=0, tiled=True)
     mine = lax.dynamic_slice_in_dim(weights, me, 1, axis=1)
-    everyone = lax.all_gather(tokens, "expert", axis=0, tiled=True)
+    workers = axis_size("expert")
+    samples = [tokens]
+    for tick in tuple(range(workers - 1)):
+        samples.append(
+            ppermute(
+                samples[-1], "expert", [(src_i, (src_i + 1) % workers) for src_i in range(workers)]
+            )
+        )
+    everyone = jnp.roll(
+        jnp.concatenate(samples[::-1], axis=0), (axis_index("expert") + 1) * tokens.shape[0], axis=0
+    )
     part = expert_mlp(everyone, w_gate[0], w_up[0], w_down[0])
     part = part.astype(jnp.bfloat16).astype(jnp.float32) * mine
     return lax.psum_scatter(part.astype(jnp.bfloat16), "expert", scatter_dimension=0, tiled=True)

time: 228 us -> 357 us (1.57)
  waiting for transfers between devices: 157 us -> 260 us
  local copies, waits for them, and re-layouts: 0.01 us -> 30.6 us
  blocking collectives: 24.1 us -> 20.4 us
    ppermute x0 -> x15, waiting for transfers between devices: none -> 159 us  [dense_on_device(): ppermute(samples[-1], 'expert', [(src_i, (src_i + 1) % workers) for src_i...]
    all_gather x1 -> x0, waiting for transfers between devices: 54.4 us -> none  [dense_on_device(): everyone = lax.all_gather(tokens, 'expert', axis=0, tiled=True)]
    unnamed x2 -> x91, local copies, waits for them, and re-layouts: 0.01 us -> 30.5 us
    all_gather x1, blocking collectives: 24.1 us -> 20.4 us  [dense_on_device(): weights = lax.all_gather(weight, 'expert', axis=0, tiled=True)]
  transfers between devices with their start and end apart: 2 -> 16, of which waited for: 2 -> 15; matrix products, arithmetic and copies ran while one was open for 0% -> 0% of each run, Pallas kernels for 0% -> 0%
where the time goes in v1:
time: 357 us; the launch traced here: 356 us
  waiting for transfers between devices  260 us (73%)
  local copies, waits for them, and re-layouts  30.6 us (9%)
  matrix products  29.3 us (8%)
  blocking collectives  20.4 us (6%)
  between operations  13.8 us (4%)
    ppermute x15, waiting for transfers between devices, dense_on_device(): ppermute(samples[-1], 'expert', [(src_i, (src_i + 1) % workers) for src_i...  159 us
    reduce_scatter x1, waiting for transfers between devices, dense_on_device(): lax.psum_scatter(part.astype(jnp.bfloat16), 'expert', scatter_dimension=0...  101 us
    unnamed x91, local copies, waits for them, and re-layouts  30.5 us
    dot_general x1, matrix products, expert_mlp(): return jnp.dot(hidden, down_local, preferred_element_type=jnp.float32)  20.8 us
    all_gather x1, blocking collectives, dense_on_device(): weights = lax.all_gather(weight, 'expert', axis=0, tiled=True)  20.4 us
    dot_general x1, matrix products, expert_mlp(): up_part = jnp.dot(block_data, up_local, preferred_element_type=jnp.float32)  8.56 us
  transfers between devices with their start and end apart: 16, of which 15 were waited for; matrix products, arithmetic and copies ran while one was open for 0% of the time, Pallas kernels for 0%

profile of v1, /device:TPU:0, one launch (start us, length us, event | category | flops | bytes accessed | tf_op | source)
XLA Modules:
  0.0 356.0 jit_solution(13927726400886991720)
XLA Ops:
  7.0 12.0 %collective-permute-done = bf16[128,2048]{1,0:T(8,128)(2,1)S(1)} collective-permute-done((bf16[128,2048]{1,0:T(8,128)(2,1)}, bf16[128,2048]{1,0:T(8,128)(2,1)S(1)}, u32[]{:S(2)}, u32[]{:S(2)}) %collective-permute-start) | collective-permute-done | bytes 524320 | tf_op jit(solution)/shard_map/ppermute | solution.py:28
  19.8 11.3 %collective-permute-done.1 = bf16[128,2048]{1,0:T(8,128)(2,1)S(1)} collective-permute-done((bf16[128,2048]{1,0:T(8,128)(2,1)S(1)}, bf16[128,2048]{1,0:T(8,128)(2,1)S(1)}, u32[]{:S(2)}, u32[]{:S(2)}) %collective-permute-start.1) | collective-permute-done | bytes 524320 | tf_op jit(solution)/shard_map/ppermute | solution.py:28
  32.0 11.3 %collective-permute-done.2 = bf16[128,2048]{1,0:T(8,128)(2,1)S(1)} collective-permute-done((bf16[128,2048]{1,0:T(8,128)(2,1)S(1)}, bf16[128,2048]{1,0:T(8,128)(2,1)S(1)}, u32[]{:S(2)}, u32[]{:S(2)}) %collective-permute-start.2) | collective-permute-done | bytes 524320 | tf_op jit(solution)/shard_map/ppermute | solution.py:28
  44.1 11.3 %collective-permute-done.3 = bf16[128,2048]{1,0:T(8,128)(2,1)S(1)} collective-permute-done((bf16[128,2048]{1,0:T(8,128)(2,1)S(1)}, bf16[128,2048]{1,0:T(8,128)(2,1)S(1)}, u32[]{:S(2)}, u32[]{:S(2)}) %collective-permute-start.3) | collective-permute-done | bytes 524320 | tf_op jit(solution)/shard_map/ppermute | solution.py:28
  56.2 11.3 %collective-permute-done.4 = bf16[128,2048]{1,0:T(8,128)(2,1)S(1)} collective-permute-done((bf16[128,2048]{1,0:T(8,128)(2,1)S(1)}, bf16[128,2048]{1,0:T(8,128)(2,1)S(1)}, u32[]{:S(2)}, u32[]{:S(2)}) %collective-permute-start.4) | collective-permute-done | bytes 524320 | tf_op jit(solution)/shard_map/ppermute | solution.py:28
  68.3 11.3 %collective-permute-done.5 = bf16[128,2048]{1,0:T(8,128)(2,1)S(1)} collective-permute-done((bf16[128,2048]{1,0:T(8,128)(2,1)S(1)}, bf16[128,2048]{1,0:T(8,128)(2,1)S(1)}, u32[]{:S(2)}, u32[]{:S(2)}) %collective-permute-start.5) | collective-permute-done | bytes 524320 | tf_op jit(solution)/shard_map/ppermute | solution.py:28
  80.4 11.3 %collective-permute-done.6 = bf16[128,2048]{1,0:T(8,128)(2,1)S(1)} collective-permute-done((bf16[128,2048]{1,0:T(8,128)(2,1)S(1)}, bf16[128,2048]{1,0:T(8,128)(2,1)S(1)}, u32[]{:S(2)}, u32[]{:S(2)}) %collective-permute-start.6) | collective-permute-done | bytes 524320 | tf_op jit(solution)/shard_map/ppermute | solution.py:28
  92.5 11.3 %collective-permute-done.7 = bf16[128,2048]{1,0:T(8,128)(2,1)S(1)} collective-permute-done((bf16[128,2048]{1,0:T(8,128)(2,1)S(1)}, bf16[128,2048]{1,0:T(8,128)(2,1)S(1)}, u32[]{:S(2)}, u32[]{:S(2)}) %collective-permute-start.7) | collective-permute-done | bytes 524320 | tf_op jit(solution)/shard_map/ppermute | solution.py:28
  104.6 11.3 %collective-permute-done.8 = bf16[128,2048]{1,0:T(8,128)(2,1)S(1)} collective-permute-done((bf16[128,2048]{1,0:T(8,128)(2,1)S(1)}, bf16[128,2048]{1,0:T(8,128)(2,1)S(1)}, u32[]{:S(2)}, u32[]{:S(2)}) %collective-permute-start.8) | collective-permute-done | bytes 524320 | tf_op jit(solution)/shard_map/ppermute | solution.py:28
  116.7 11.3 %collective-permute-done.9 = bf16[128,2048]{1,0:T(8,128)(2,1)S(1)} collective-permute-done((bf16[128,2048]{1,0:T(8,128)(2,1)S(1)}, bf16[128,2048]{1,0:T(8,128)(2,1)S(1)}, u32[]{:S(2)}, u32[]{:S(2)}) %collective-permute-start.9) | collective-permute-done | bytes 524320 | tf_op jit(solution)/shard_map/ppermute | solution.py:28
  128.9 11.3 %collective-permute-done.10 = bf16[128,2048]{1,0:T(8,128)(2,1)S(1)} collective-permute-done((bf16[128,2048]{1,0:T(8,128)(2,1)S(1)}, bf16[128,2048]{1,0:T(8,128)(2,1)S(1)}, u32[]{:S(2)}, u32[]{:S(2)}) %collective-permute-start.10) | collective-permute-done | bytes 524320 | tf_op jit(solution)/shard_map/ppermute | solution.py:28
  141.0 11.3 %collective-permute-done.11 = bf16[128,2048]{1,0:T(8,128)(2,1)S(1)} collective-permute-done((bf16[128,2048]{1,0:T(8,128)(2,1)S(1)}, bf16[128,2048]{1,0:T(8,128)(2,1)S(1)}, u32[]{:S(2)}, u32[]{:S(2)}) %collective-permute-start.11) | collective-permute-done | bytes 524320 | tf_op jit(solution)/shard_map/ppermute | solution.py:28
  153.1 11.3 %collective-permute-done.12 = bf16[128,2048]{1,0:T(8,128)(2,1)S(1)} collective-permute-done((bf16[128,2048]{1,0:T(8,128)(2,1)S(1)}, bf16[128,2048]{1,0:T(8,128)(2,1)S(1)}, u32[]{:S(2)}, u32[]{:S(2)}) %collective-permute-start.12) | collective-permute-done | bytes 524320 | tf_op jit(solution)/shard_map/ppermute | solution.py:28
  165.2 11.5 %collective-permute-done.13 = bf16[128,2048]{1,0:T(8,128)(2,1)} collective-permute-done((bf16[128,2048]{1,0:T(8,128)(2,1)S(1)}, bf16[128,2048]{1,0:T(8,128)(2,1)}, u32[]{:S(2)}, u32[]{:S(2)}) %collective-permute-start.13) | collective-permute-done | bytes 524320 | tf_op jit(solution)/shard_map/ppermute | solution.py:28
  177.7 20.4 %all_gather.3 = f32[2048,16]{0,1:T(8,128)S(1)} all-gather(f32[128,16]{0,1:T(8,128)S(1)} %select_reduce_fusion), channel_id=1, replica_groups=mesh['groups'=2,'expert'=16] {'expert'}, dimensions={0}, use_global_device_ids=true | all-gather | bytes 139264 | tf_op jit(solution)/shard_map/all_gather | solution.py:22
  198.1 1.2 constant_dynamic-update-slice_fusion.31
  199.3 1.1 constant_dynamic-update-slice_fusion.30
  200.4 1.1 constant_dynamic-update-slice_fusion.29
  208.0 1.1 constant_dynamic-update-slice_fusion.22
  209.1 1.1 constant_dynamic-update-slice_fusion.21
  214.5 1.1 constant_dynamic-update-slice_fusion.16
  218.5 8.6 %fusion = f32[2048,768]{1,0:T(8,128)} fusion(bf16[4096,2048]{1,0:T(8,128)(2,1)S(1)} %constant_dynamic-update-slice_fusion, s32[]{:T(128)S(6)} %select_n.21, bf16[1,2048,768]{2,1,0:T(8,128)(2,1)S(1)} %copy-done.29), kind=kOutput, calls=%fused_computation.1 | convolution fusion | flops 6442450944 | bytes 17825796 | tf_op jit(solution)/shard_map/dot_general | solution.py:10
  227.1 20.8 %multiply_convert_fusion = bf16[2048,2048]{1,0:T(8,128)(2,1)} fusion(f32[2048]{0:T(1024)S(1)} %bitcast.11, f32[2048,768]{1,0:T(8,128)} %fusion, bf16[4096,2048]{1,0:T(8,128)(2,1)} %copy-done.28, s32[]{:T(128)S(6)} %select_n.21, bf16[1,768,2048]{2,1,0:T(8,128)(2,1)S(1)} %copy-done, bf16[1,2048,768]{2,1,0:T(8,128)(2,1)} %param.9), kind=kOutput, calls=%fused_computation | convolution fusion | flops 12911116288 | bytes 29368324 | tf_op jit(solution)/shard_map/dot_general | solution.py:12
  247.8 101.3 %reduce-scatter.2.cloned.1.call-done = bf16[128,2048]{1,0:T(8,128)(2,1)} async-done(((bf16[2048,2048]{1,0:T(8,128)(2,1)}), bf16[128,2048]{1,0:T(8,128)(2,1)}) %reduce-scatter.2.cloned.1.call-update) | async-done | bytes 524304 | tf_op jit(solution)/shard_map/reduce_scatter | solution.py:37
  (106 shorter events, 25.4 us)
Async XLA Ops:
  6.5 220.5 %copy-start = (bf16[1,768,2048]{2,1,0:T(8,128)(2,1)S(1)}, bf16[1,768,2048]{2,1,0:T(8,128)(2,1)}, u32[]{:S(2)}) copy-start(bf16[1,768,2048]{2,1,0:T(8,128)(2,1)} %param.11) | copy-start | bytes 9437188
  6.5 342.6 %reduce-scatter.2.cloned.1.call-start = ((), (), s32[]{:S(2)}) async-start(), calls=%async_computation.1 | async-start | bytes 8912896 | tf_op jit(solution)/shard_map/reduce_scatter | solution.py:37
  6.5 12.5 %collective-permute-start = (bf16[128,2048]{1,0:T(8,128)(2,1)}, bf16[128,2048]{1,0:T(8,128)(2,1)S(1)}, u32[]{:S(2)}, u32[]{:S(2)}) collective-permute-start(bf16[128,2048]{1,0:T(8,128)(2,1)} %param.6), channel_id=1, source_target_pairs={{0,1},{1,2},{2,3},{3,4},{4,5},{5,6},{6,7},{7,8},{8,9},{9,10},{10,1... | collective-permute-start | bytes 1572872 | tf_op jit(solution)/shard_map/ppermute | solution.py:28
  19.8 11.3 %collective-permute-start.1 = (bf16[128,2048]{1,0:T(8,128)(2,1)S(1)}, bf16[128,2048]{1,0:T(8,128)(2,1)S(1)}, u32[]{:S(2)}, u32[]{:S(2)}) collective-permute-start(bf16[128,2048]{1,0:T(8,128)(2,1)S(1)} %collective-permute-done), channel_id=1, source_target_pairs={{0,1},{1,2},{2,3},{3,4},{4,5},{5,6},{6,7},{7,8},{8,9},{9,10},{10,1... | collective-permute-start | bytes 1572872 | tf_op jit(solution)/shard_map/ppermute | solution.py:28
  32.0 11.3 %collective-permute-start.2 = (bf16[128,2048]{1,0:T(8,128)(2,1)S(1)}, bf16[128,2048]{1,0:T(8,128)(2,1)S(1)}, u32[]{:S(2)}, u32[]{:S(2)}) collective-permute-start(bf16[128,2048]{1,0:T(8,128)(2,1)S(1)} %collective-permute-done.1), channel_id=1, source_target_pairs={{0,1},{1,2},{2,3},{3,4},{4,5},{5,6},{6,7},{7,8},{8,9},{9,10},{10,1... | collective-permute-start | bytes 1572872 | tf_op jit(solution)/shard_map/ppermute | solution.py:28
  44.1 11.3 %collective-permute-start.3 = (bf16[128,2048]{1,0:T(8,128)(2,1)S(1)}, bf16[128,2048]{1,0:T(8,128)(2,1)S(1)}, u32[]{:S(2)}, u32[]{:S(2)}) collective-permute-start(bf16[128,2048]{1,0:T(8,128)(2,1)S(1)} %collective-permute-done.2), channel_id=1, source_target_pairs={{0,1},{1,2},{2,3},{3,4},{4,5},{5,6},{6,7},{7,8},{8,9},{9,10},{10,1... | collective-permute-start | bytes 1572872 | tf_op jit(solution)/shard_map/ppermute | solution.py:28
  56.2 11.3 %collective-permute-start.4 = (bf16[128,2048]{1,0:T(8,128)(2,1)S(1)}, bf16[128,2048]{1,0:T(8,128)(2,1)S(1)}, u32[]{:S(2)}, u32[]{:S(2)}) collective-permute-start(bf16[128,2048]{1,0:T(8,128)(2,1)S(1)} %collective-permute-done.3), channel_id=1, source_target_pairs={{0,1},{1,2},{2,3},{3,4},{4,5},{5,6},{6,7},{7,8},{8,9},{9,10},{10,1... | collective-permute-start | bytes 1572872 | tf_op jit(solution)/shard_map/ppermute | solution.py:28
  68.3 11.3 %collective-permute-start.5 = (bf16[128,2048]{1,0:T(8,128)(2,1)S(1)}, bf16[128,2048]{1,0:T(8,128)(2,1)S(1)}, u32[]{:S(2)}, u32[]{:S(2)}) collective-permute-start(bf16[128,2048]{1,0:T(8,128)(2,1)S(1)} %collective-permute-done.4), channel_id=1, source_target_pairs={{0,1},{1,2},{2,3},{3,4},{4,5},{5,6},{6,7},{7,8},{8,9},{9,10},{10,1... | collective-permute-start | bytes 1572872 | tf_op jit(solution)/shard_map/ppermute | solution.py:28
  80.4 11.3 %collective-permute-start.6 = (bf16[128,2048]{1,0:T(8,128)(2,1)S(1)}, bf16[128,2048]{1,0:T(8,128)(2,1)S(1)}, u32[]{:S(2)}, u32[]{:S(2)}) collective-permute-start(bf16[128,2048]{1,0:T(8,128)(2,1)S(1)} %collective-permute-done.5), channel_id=1, source_target_pairs={{0,1},{1,2},{2,3},{3,4},{4,5},{5,6},{6,7},{7,8},{8,9},{9,10},{10,1... | collective-permute-start | bytes 1572872 | tf_op jit(solution)/shard_map/ppermute | solution.py:28
  92.5 11.3 %collective-permute-start.7 = (bf16[128,2048]{1,0:T(8,128)(2,1)S(1)}, bf16[128,2048]{1,0:T(8,128)(2,1)S(1)}, u32[]{:S(2)}, u32[]{:S(2)}) collective-permute-start(bf16[128,2048]{1,0:T(8,128)(2,1)S(1)} %collective-permute-done.6), channel_id=1, source_target_pairs={{0,1},{1,2},{2,3},{3,4},{4,5},{5,6},{6,7},{7,8},{8,9},{9,10},{10,1... | collective-permute-start | bytes 1572872 | tf_op jit(solution)/shard_map/ppermute | solution.py:28
  104.6 11.3 %collective-permute-start.8 = (bf16[128,2048]{1,0:T(8,128)(2,1)S(1)}, bf16[128,2048]{1,0:T(8,128)(2,1)S(1)}, u32[]{:S(2)}, u32[]{:S(2)}) collective-permute-start(bf16[128,2048]{1,0:T(8,128)(2,1)S(1)} %collective-permute-done.7), channel_id=1, source_target_pairs={{0,1},{1,2},{2,3},{3,4},{4,5},{5,6},{6,7},{7,8},{8,9},{9,10},{10,1... | collective-permute-start | bytes 1572872 | tf_op jit(solution)/shard_map/ppermute | solution.py:28
  116.7 11.3 %collective-permute-start.9 = (bf16[128,2048]{1,0:T(8,128)(2,1)S(1)}, bf16[128,2048]{1,0:T(8,128)(2,1)S(1)}, u32[]{:S(2)}, u32[]{:S(2)}) collective-permute-start(bf16[128,2048]{1,0:T(8,128)(2,1)S(1)} %collective-permute-done.8), channel_id=1, source_target_pairs={{0,1},{1,2},{2,3},{3,4},{4,5},{5,6},{6,7},{7,8},{8,9},{9,10},{10,1... | collective-permute-start | bytes 1572872 | tf_op jit(solution)/shard_map/ppermute | solution.py:28
  128.8 11.3 %collective-permute-start.10 = (bf16[128,2048]{1,0:T(8,128)(2,1)S(1)}, bf16[128,2048]{1,0:T(8,128)(2,1)S(1)}, u32[]{:S(2)}, u32[]{:S(2)}) collective-permute-start(bf16[128,2048]{1,0:T(8,128)(2,1)S(1)} %collective-permute-done.9), channel_id=1, source_target_pairs={{0,1},{1,2},{2,3},{3,4},{4,5},{5,6},{6,7},{7,8},{8,9},{9,10},{10,1... | collective-permute-start | bytes 1572872 | tf_op jit(solution)/shard_map/ppermute | solution.py:28
  140.9 11.3 %collective-permute-start.11 = (bf16[128,2048]{1,0:T(8,128)(2,1)S(1)}, bf16[128,2048]{1,0:T(8,128)(2,1)S(1)}, u32[]{:S(2)}, u32[]{:S(2)}) collective-permute-start(bf16[128,2048]{1,0:T(8,128)(2,1)S(1)} %collective-permute-done.10), channel_id=1, source_target_pairs={{0,1},{1,2},{2,3},{3,4},{4,5},{5,6},{6,7},{7,8},{8,9},{9,10},{10,1... | collective-permute-start | bytes 1572872 | tf_op jit(solution)/shard_map/ppermute | solution.py:28
  153.1 11.3 %collective-permute-start.12 = (bf16[128,2048]{1,0:T(8,128)(2,1)S(1)}, bf16[128,2048]{1,0:T(8,128)(2,1)S(1)}, u32[]{:S(2)}, u32[]{:S(2)}) collective-permute-start(bf16[128,2048]{1,0:T(8,128)(2,1)S(1)} %collective-permute-done.11), channel_id=1, source_target_pairs={{0,1},{1,2},{2,3},{3,4},{4,5},{5,6},{6,7},{7,8},{8,9},{9,10},{10,1... | collective-permute-start | bytes 1572872 | tf_op jit(solution)/shard_map/ppermute | solution.py:28
  165.2 11.5 %collective-permute-start.13 = (bf16[128,2048]{1,0:T(8,128)(2,1)S(1)}, bf16[128,2048]{1,0:T(8,128)(2,1)}, u32[]{:S(2)}, u32[]{:S(2)}) collective-permute-start(bf16[128,2048]{1,0:T(8,128)(2,1)S(1)} %collective-permute-done.12), channel_id=1, source_target_pairs={{0,1},{1,2},{2,3},{3,4},{4,5},{5,6},{6,7},{7,8},{8,9},{9,10},{10,1... | collective-permute-start | bytes 1572872 | tf_op jit(solution)/shard_map/ppermute | solution.py:28
  176.7 21.4 %collective-permute-start.14 = (bf16[128,2048]{1,0:T(8,128)(2,1)}, bf16[128,2048]{1,0:T(8,128)(2,1)}, u32[]{:S(2)}, u32[]{:S(2)}) collective-permute-start(bf16[128,2048]{1,0:T(8,128)(2,1)} %collective-permute-done.13), channel_id=1, source_target_pairs={{0,1},{1,2},{2,3},{3,4},{4,5},{5,6},{6,7},{7,8},{8,9},{9,10},{10,1... | collective-permute-start | bytes 1572872 | tf_op jit(solution)/shard_map/ppermute | solution.py:28
  176.7 41.4 %copy-start.13 = (bf16[128,2048]{1,0:T(8,128)(2,1)S(1)}, bf16[128,2048]{1,0:T(8,128)(2,1)}, u32[]{:S(2)}) copy-start(bf16[128,2048]{1,0:T(8,128)(2,1)} %copy-done.12) | copy-start | bytes 1572868
  176.7 41.4 %copy-start.11 = (bf16[128,2048]{1,0:T(8,128)(2,1)S(1)}, bf16[128,2048]{1,0:T(8,128)(2,1)}, u32[]{:S(2)}) copy-start(bf16[128,2048]{1,0:T(8,128)(2,1)} %copy-done.10) | copy-start | bytes 1572868
  176.7 41.5 %copy-start.9 = (bf16[128,2048]{1,0:T(8,128)(2,1)S(1)}, bf16[128,2048]{1,0:T(8,128)(2,1)}, u32[]{:S(2)}) copy-start(bf16[128,2048]{1,0:T(8,128)(2,1)} %copy-done.8) | copy-start | bytes 1572868
  176.7 41.5 %copy-start.7 = (bf16[128,2048]{1,0:T(8,128)(2,1)S(1)}, bf16[128,2048]{1,0:T(8,128)(2,1)}, u32[]{:S(2)}) copy-start(bf16[128,2048]{1,0:T(8,128)(2,1)} %copy-done.6) | copy-start | bytes 1572868
  176.8 41.6 %copy-start.5 = (bf16[128,2048]{1,0:T(8,128)(2,1)S(1)}, bf16[128,2048]{1,0:T(8,128)(2,1)}, u32[]{:S(2)}) copy-start(bf16[128,2048]{1,0:T(8,128)(2,1)} %copy-done.4) | copy-start | bytes 1572868
  176.8 41.6 %copy-start.3 = (bf16[128,2048]{1,0:T(8,128)(2,1)S(1)}, bf16[128,2048]{1,0:T(8,128)(2,1)}, u32[]{:S(2)}) copy-start(bf16[128,2048]{1,0:T(8,128)(2,1)} %copy-done.2) | copy-start | bytes 1572868
  176.8 41.6 %copy-start.1 = (bf16[128,2048]{1,0:T(8,128)(2,1)S(1)}, bf16[128,2048]{1,0:T(8,128)(2,1)}, u32[]{:S(2)}) copy-start(bf16[128,2048]{1,0:T(8,128)(2,1)} %param.6) | copy-start | bytes 1572868
  (22 other events, 327.8 us)
Sparse Core Ops, SparseCore 0:
  248.0 101.1 reduce-scatter.1
